TPU v7x, 512 devices: a whole 4x4x16 slice. The times are simulated.
512 devices in a mesh: blk: 128 (over z_lo, y, x), off: 4 (over z_hi, core).
Axes of the slice: x: 4, y: 4, z: 16 (z_hi: 2, z_lo: 8; z = z_hi * 8 + z_lo), core: 2. Of those that a mesh axis runs over, the one named last changes fastest.
Arguments:
- coefficients: bfloat16 [2048, 32, 128], P('blk', 'off'), may hold values from -12 to 12
Outputs:
- smoothed: float32 [2048, 32, 128], P(('blk', 'off'))
- log_degree: float32 [2048], P(('blk', 'off'))
All inputs are finite; a program needn't handle non-finite values.
Results may differ from a plain program's by a relative error of at most 0.005.
Values may be sent and summed in bfloat16 or wider, within the bound.
A program may use at most 64 MiB of HBM per device.

v0:
```python
import math
import jax
import jax.numpy as jnp
from jax import lax
from jax.sharding import PartitionSpec as P

epsilon = 1e-06
concentration = 40.0


def shifted(array, axis, by):
    count = lax.axis_size(axis)
    return lax.ppermute(array, axis, [(i, (i + by) % count) for i in range(count)])


def angle_tables(angular):
    half_width = angular // 2
    frequency = jnp.arange(half_width, dtype=jnp.int32)
    shifts = jnp.arange(angular, dtype=jnp.int32)
    product = frequency[:, None] * shifts[None, :] % angular
    phase = product.astype(jnp.float32) * (2.0 * math.pi / angular)
    forward = jnp.concatenate([jnp.cos(phase), -jnp.sin(phase)], axis=0)
    return (forward, forward.T)


def inverse_norms(block_values):
    values = block_values.astype(jnp.float32)
    return lax.rsqrt(jnp.sum(values * values, axis=(1, 2)) + epsilon)


def tile_terms(own_block, own_inverse, other_block, offset, forward, backward):
    row_count = own_block.shape[0]
    half_width = own_block.shape[2] // 2
    highest = lax.Precision.HIGHEST
    other_inverse = inverse_norms(other_block)
    swapped = jnp.concatenate(
        [other_block[:, :, half_width:], other_block[:, :, :half_width]], axis=2
    )
    direct = jnp.einsum("irc,jrc->ijc", own_block, other_block, preferred_element_type=jnp.float32)
    mixed_terms = jnp.einsum("irc,jrc->ijc", own_block, swapped, preferred_element_type=jnp.float32)
    real_part = direct[:, :, :half_width] + direct[:, :, half_width:]
    imag_part = mixed_terms[:, :, half_width:] - mixed_terms[:, :, :half_width]
    cross_spectrum = jnp.concatenate([real_part, imag_part], axis=2).reshape(
        row_count * row_count, -1
    )
    correlation = jnp.dot(
        cross_spectrum, forward, precision=highest, preferred_element_type=jnp.float32
    )
    correlation = correlation.reshape(row_count, row_count, -1)
    cosine = correlation * own_inverse[:, None, None] * other_inverse[None, :, None]
    same_image = jnp.arange(row_count)[:, None] == jnp.arange(row_count)[None, :]
    keep_mask = jnp.where(jnp.logical_and(offset == 0, same_image), 0.0, 1.0).astype(jnp.float32)
    weights = jnp.exp(concentration * cosine) * keep_mask[:, :, None]
    spectral = jnp.dot(
        weights.reshape(row_count * row_count, -1),
        backward,
        precision=highest,
        preferred_element_type=jnp.float32,
    ).reshape(row_count, row_count, -1)
    degree = jnp.sum(spectral[:, :, 0], axis=1)
    rounded = spectral.astype(jnp.bfloat16)
    weight_real = jnp.concatenate([rounded[:, :, :half_width], rounded[:, :, :half_width]], axis=2)
    weight_imag = jnp.concatenate([-rounded[:, :, half_width:], rounded[:, :, half_width:]], axis=2)
    filtered = jnp.einsum(
        "ijc,jrc->irc", weight_real, other_block, preferred_element_type=jnp.float32
    )
    filtered = filtered + jnp.einsum(
        "ijc,jrc->irc", weight_imag, swapped, preferred_element_type=jnp.float32
    )
    return (filtered, degree)


def body(coefficients):
    own_block = lax.all_gather(coefficients, "off", axis=1, tiled=True)
    own_inverse = inverse_norms(own_block)
    row_count, radial, angular = own_block.shape
    forward, backward = angle_tables(angular)
    ranges = lax.axis_size("off")
    per_range = min(8, lax.axis_size("blk") // ranges)
    range_index = lax.axis_index("off")
    range_base = range_index * per_range
    packet = own_block
    for bit_number in range(ranges.bit_length() - 1):
        moved_packet = shifted(packet, "blk", -(per_range << bit_number))
        chosen = range_index // (1 << bit_number) % 2 == 1
        packet = jnp.where(chosen, moved_packet, packet)
    empty_sum = jnp.zeros((row_count, radial, angular), jnp.float32)
    empty_degree = jnp.zeros((row_count,), jnp.float32)

    def advance_one(step, loop_state):
        filtered, degree, current = loop_state
        terms = tile_terms(own_block, own_inverse, current, range_base + step, forward, backward)
        current = shifted(current, "blk", -1)
        return (filtered + terms[0], degree + terms[1], current)

    last_step = per_range - 1
    filtered, degree, current = lax.fori_loop(
        0, last_step, advance_one, (empty_sum, empty_degree, packet)
    )
    terms = tile_terms(own_block, own_inverse, current, range_base + last_step, forward, backward)
    filtered = filtered + terms[0]
    degree = degree + terms[1]
    totals = (
        lax.psum_scatter(filtered, "off", scatter_dimension=0, tiled=True),
        lax.psum_scatter(degree, "off", scatter_dimension=0, tiled=True),
    )
    smoothed = totals[0] / totals[1][:, None, None]
    return (smoothed, jnp.log(totals[1]))


def solution(mesh):
    return jax.shard_map(
        body,
        mesh=mesh,
        in_specs=(P("blk", "off", None),),
        out_specs=(P(("blk", "off"), None, None), P(("blk", "off"))),
        check_vma=False,
    )
```

profile of v0, /device:TPU:1, one launch (start us, length us, event | category | flops | bytes accessed | tf_op | source)
XLA Modules:
  0.0 278.7 jit_solution(10738338174467296353)
XLA Ops:
  8.2 28.6 %all_gather.3 = bf16[16,32,128]{0,1,2:T(8,128)(2,1)S(1)} all-gather(bf16[16,8,128]{0,1,2:T(8,128)(2,1)S(1)} %copy.20), channel_id=1, replica_groups=mesh['blk'=128,'off'=4] {'off'}, dimensions={1}, use_global_device_ids=true | all-gather | bytes 163840 | tf_op jit(solution)/shard_map/all_gather | solution.py:74
  38.0 14.6 %collective-permute-start.1 = (bf16[16,32,128]{2,1,0:T(8,128)(2,1)S(1)}, bf16[16,32,128]{2,1,0:T(8,128)(2,1)S(1)}, u32[]{:S(2)}, u32[]{:S(2)}) collective-permute-start(bf16[16,32,128]{2,1,0:T(8,128)(2,1)S(1)} %copy.21), channel_id=1, source_target_pairs={{0,480},{4,484},{8,488},{12,492},{16,496},{20,500},{24,504},{28,50... | collective-permute-start | bytes 393224 | tf_op jit(solution)/shard_map/ppermute | solution.py:13
  53.4 1.9 collective-permute-done.1
  55.3 2.4 copy.22
  60.2 9.7 %collective-permute-start.2 = (bf16[16,32,128]{2,1,0:T(8,128)(2,1)S(1)}, bf16[16,32,128]{2,1,0:T(8,128)(2,1)S(1)}, u32[]{:S(2)}, u32[]{:S(2)}) collective-permute-start(bf16[16,32,128]{2,1,0:T(8,128)(2,1)S(1)} %copy.23), channel_id=1, source_target_pairs={{0,448},{4,452},{8,456},{12,460},{16,464},{20,468},{24,472},{28,47... | collective-permute-start | bytes 393224 | tf_op jit(solution)/shard_map/ppermute | solution.py:13
  71.2 1.8 collective-permute-done.2
  75.6 2.5 copy.25
  78.1 125.4 %while.18 = (s32[]{:T(128)}, f32[16,32,128]{1,0,2:T(8,128)}, f32[16]{0:T(128)}, bf16[16,32,128]{2,1,0:T(8,128)(2,1)S(1)}, bf16[16,32,128]{1,0,2:T(8,128)(2,1)S(1...) while((s32[]{:T(128)}, f32[16,32,128]{1,0,2:T(8,128)}, ...), condition=%wide.region_4.5_spmd.clone, body=%wide.region_1.4_spmd.clone.sunk | while | flops 110216208 | bytes 6230326 | solution.py:97
  78.3 16.1 %collective-permute-start = (bf16[16,32,128]{2,1,0:T(8,128)(2,1)S(1)}, bf16[16,32,128]{2,1,0:T(8,128)(2,1)S(1)}, u32[]{:S(2)}, u32[]{:S(2)}) collective-permute-start(bf16[16,32,128]{2,1,0:T(8,128)(2,1)S(1)} %copy.56), channel_id=1, source_target_pairs={{0,508},{4,0},{8,4},{12,8},{16,12},{20,16},{24,20},{28,24},{32,28}... | collective-permute-start | bytes 393224 | tf_op jit(solution)/shard_map/while/body/eval_jaxpr/ppermute | solution.py:13
  102.4 9.1 %collective-permute-start = (bf16[16,32,128]{2,1,0:T(8,128)(2,1)S(1)}, bf16[16,32,128]{2,1,0:T(8,128)(2,1)S(1)}, u32[]{:S(2)}, u32[]{:S(2)}) collective-permute-start(bf16[16,32,128]{2,1,0:T(8,128)(2,1)S(1)} %copy.56), channel_id=1, source_target_pairs={{0,508},{4,0},{8,4},{12,8},{16,12},{20,16},{24,20},{28,24},{32,28}... | collective-permute-start | bytes 393224 | tf_op jit(solution)/shard_map/while/body/eval_jaxpr/ppermute | solution.py:13
  117.5 2.7 fusion.95
  120.8 7.3 %collective-permute-start = (bf16[16,32,128]{2,1,0:T(8,128)(2,1)S(1)}, bf16[16,32,128]{2,1,0:T(8,128)(2,1)S(1)}, u32[]{:S(2)}, u32[]{:S(2)}) collective-permute-start(bf16[16,32,128]{2,1,0:T(8,128)(2,1)S(1)} %copy.56), channel_id=1, source_target_pairs={{0,508},{4,0},{8,4},{12,8},{16,12},{20,16},{24,20},{28,24},{32,28}... | collective-permute-start | bytes 393224 | tf_op jit(solution)/shard_map/while/body/eval_jaxpr/ppermute | solution.py:13
  134.1 2.7 fusion.95
  137.3 7.3 %collective-permute-start = (bf16[16,32,128]{2,1,0:T(8,128)(2,1)S(1)}, bf16[16,32,128]{2,1,0:T(8,128)(2,1)S(1)}, u32[]{:S(2)}, u32[]{:S(2)}) collective-permute-start(bf16[16,32,128]{2,1,0:T(8,128)(2,1)S(1)} %copy.56), channel_id=1, source_target_pairs={{0,508},{4,0},{8,4},{12,8},{16,12},{20,16},{24,20},{28,24},{32,28}... | collective-permute-start | bytes 393224 | tf_op jit(solution)/shard_map/while/body/eval_jaxpr/ppermute | solution.py:13
  150.6 2.7 fusion.95
  153.9 7.3 %collective-permute-start = (bf16[16,32,128]{2,1,0:T(8,128)(2,1)S(1)}, bf16[16,32,128]{2,1,0:T(8,128)(2,1)S(1)}, u32[]{:S(2)}, u32[]{:S(2)}) collective-permute-start(bf16[16,32,128]{2,1,0:T(8,128)(2,1)S(1)} %copy.56), channel_id=1, source_target_pairs={{0,508},{4,0},{8,4},{12,8},{16,12},{20,16},{24,20},{28,24},{32,28}... | collective-permute-start | bytes 393224 | tf_op jit(solution)/shard_map/while/body/eval_jaxpr/ppermute | solution.py:13
  167.2 2.7 fusion.95
  170.5 7.3 %collective-permute-start = (bf16[16,32,128]{2,1,0:T(8,128)(2,1)S(1)}, bf16[16,32,128]{2,1,0:T(8,128)(2,1)S(1)}, u32[]{:S(2)}, u32[]{:S(2)}) collective-permute-start(bf16[16,32,128]{2,1,0:T(8,128)(2,1)S(1)} %copy.56), channel_id=1, source_target_pairs={{0,508},{4,0},{8,4},{12,8},{16,12},{20,16},{24,20},{28,24},{32,28}... | collective-permute-start | bytes 393224 | tf_op jit(solution)/shard_map/while/body/eval_jaxpr/ppermute | solution.py:13
  183.7 2.7 fusion.95
  187.0 7.3 %collective-permute-start = (bf16[16,32,128]{2,1,0:T(8,128)(2,1)S(1)}, bf16[16,32,128]{2,1,0:T(8,128)(2,1)S(1)}, u32[]{:S(2)}, u32[]{:S(2)}) collective-permute-start(bf16[16,32,128]{2,1,0:T(8,128)(2,1)S(1)} %copy.56), channel_id=1, source_target_pairs={{0,508},{4,0},{8,4},{12,8},{16,12},{20,16},{24,20},{28,24},{32,28}... | collective-permute-start | bytes 393224 | tf_op jit(solution)/shard_map/while/body/eval_jaxpr/ppermute | solution.py:13
  200.3 2.7 fusion.95
  210.1 1.6 fusion.17
  215.0 21.4 %all-reduce = f32[16]{0:T(128)S(1)} all-reduce(f32[16]{0:T(128)S(1)} %add.125), channel_id=3, replica_groups=mesh['blk'=128,'off'=4] {'off'}, use_global_device_ids=true, to_apply=%region_8.9.clone | all-reduce | flops 16 | bytes 128
  237.0 33.3 %reduce-scatter.2.cloned.1.call-done = f32[4,32,128]{2,1,0:T(8,128)} async-done(((f32[16,32,128]{2,1,0:T(8,128)}), f32[4,32,128]{2,1,0:T(8,128)}) %reduce-scatter.2.cloned.1.call-update) | async-done | bytes 65552 | tf_op jit(solution)/shard_map/reduce_scatter | solution.py:104
  (256 shorter events, 66.7 us)
Async XLA Ops:
  7.2 263.1 %reduce-scatter.2.cloned.1.call-start = ((), (), s32[]{:S(2)}) async-start(), calls=%async_computation.1 | async-start | bytes 327680 | tf_op jit(solution)/shard_map/reduce_scatter | solution.py:104
  36.8 33.2 %copy-start = (bf16[16,32,128]{0,1,2:T(8,128)(2,1)}, bf16[16,32,128]{0,1,2:T(8,128)(2,1)S(1)}, u32[]{:S(2)}) copy-start(bf16[16,32,128]{0,1,2:T(8,128)(2,1)S(1)} %all_gather.3) | copy-start | bytes 393220
  38.0 17.3 %collective-permute-start.1 = (bf16[16,32,128]{2,1,0:T(8,128)(2,1)S(1)}, bf16[16,32,128]{2,1,0:T(8,128)(2,1)S(1)}, u32[]{:S(2)}, u32[]{:S(2)}) collective-permute-start(bf16[16,32,128]{2,1,0:T(8,128)(2,1)S(1)} %copy.21), channel_id=1, source_target_pairs={{0,480},{4,484},{8,488},{12,492},{16,496},{20,500},{24,504},{28,50... | collective-permute-start | bytes 393224 | tf_op jit(solution)/shard_map/ppermute | solution.py:13
  53.3 16.6 %copy-start.3 = (f32[64,128]{1,0:T(8,128)}, f32[64,128]{1,0:T(8,128)S(1)}, u32[]{:S(2)}) copy-start(f32[64,128]{1,0:T(8,128)S(1)} %get-tuple-element.249) | copy-start | bytes 98308
  53.3 16.6 %copy-start.5 = (f32[64,128]{1,0:T(8,128)}, f32[64,128]{1,0:T(8,128)S(1)}, u32[]{:S(2)}) copy-start(f32[64,128]{1,0:T(8,128)S(1)} %get-tuple-element.250) | copy-start | bytes 98308
  60.2 12.8 %collective-permute-start.2 = (bf16[16,32,128]{2,1,0:T(8,128)(2,1)S(1)}, bf16[16,32,128]{2,1,0:T(8,128)(2,1)S(1)}, u32[]{:S(2)}, u32[]{:S(2)}) collective-permute-start(bf16[16,32,128]{2,1,0:T(8,128)(2,1)S(1)} %copy.23), channel_id=1, source_target_pairs={{0,448},{4,452},{8,456},{12,460},{16,464},{20,468},{24,472},{28,47... | collective-permute-start | bytes 393224 | tf_op jit(solution)/shard_map/ppermute | solution.py:13
  78.3 23.6 %collective-permute-start = (bf16[16,32,128]{2,1,0:T(8,128)(2,1)S(1)}, bf16[16,32,128]{2,1,0:T(8,128)(2,1)S(1)}, u32[]{:S(2)}, u32[]{:S(2)}) collective-permute-start(bf16[16,32,128]{2,1,0:T(8,128)(2,1)S(1)} %copy.56), channel_id=1, source_target_pairs={{0,508},{4,0},{8,4},{12,8},{16,12},{20,16},{24,20},{28,24},{32,28}... | collective-permute-start | bytes 393224 | tf_op jit(solution)/shard_map/while/body/eval_jaxpr/ppermute | solution.py:13
  100.4 1.5 copy-start.7
  102.4 17.8 %collective-permute-start = (bf16[16,32,128]{2,1,0:T(8,128)(2,1)S(1)}, bf16[16,32,128]{2,1,0:T(8,128)(2,1)S(1)}, u32[]{:S(2)}, u32[]{:S(2)}) collective-permute-start(bf16[16,32,128]{2,1,0:T(8,128)(2,1)S(1)} %copy.56), channel_id=1, source_target_pairs={{0,508},{4,0},{8,4},{12,8},{16,12},{20,16},{24,20},{28,24},{32,28}... | collective-permute-start | bytes 393224 | tf_op jit(solution)/shard_map/while/body/eval_jaxpr/ppermute | solution.py:13
  117.5 2.7 copy-start.7
  120.8 16.0 %collective-permute-start = (bf16[16,32,128]{2,1,0:T(8,128)(2,1)S(1)}, bf16[16,32,128]{2,1,0:T(8,128)(2,1)S(1)}, u32[]{:S(2)}, u32[]{:S(2)}) collective-permute-start(bf16[16,32,128]{2,1,0:T(8,128)(2,1)S(1)} %copy.56), channel_id=1, source_target_pairs={{0,508},{4,0},{8,4},{12,8},{16,12},{20,16},{24,20},{28,24},{32,28}... | collective-permute-start | bytes 393224 | tf_op jit(solution)/shard_map/while/body/eval_jaxpr/ppermute | solution.py:13
  134.1 2.7 copy-start.7
  137.3 16.0 %collective-permute-start = (bf16[16,32,128]{2,1,0:T(8,128)(2,1)S(1)}, bf16[16,32,128]{2,1,0:T(8,128)(2,1)S(1)}, u32[]{:S(2)}, u32[]{:S(2)}) collective-permute-start(bf16[16,32,128]{2,1,0:T(8,128)(2,1)S(1)} %copy.56), channel_id=1, source_target_pairs={{0,508},{4,0},{8,4},{12,8},{16,12},{20,16},{24,20},{28,24},{32,28}... | collective-permute-start | bytes 393224 | tf_op jit(solution)/shard_map/while/body/eval_jaxpr/ppermute | solution.py:13
  150.6 2.7 copy-start.7
  153.9 16.0 %collective-permute-start = (bf16[16,32,128]{2,1,0:T(8,128)(2,1)S(1)}, bf16[16,32,128]{2,1,0:T(8,128)(2,1)S(1)}, u32[]{:S(2)}, u32[]{:S(2)}) collective-permute-start(bf16[16,32,128]{2,1,0:T(8,128)(2,1)S(1)} %copy.56), channel_id=1, source_target_pairs={{0,508},{4,0},{8,4},{12,8},{16,12},{20,16},{24,20},{28,24},{32,28}... | collective-permute-start | bytes 393224 | tf_op jit(solution)/shard_map/while/body/eval_jaxpr/ppermute | solution.py:13
  167.2 2.7 copy-start.7
  170.5 16.0 %collective-permute-start = (bf16[16,32,128]{2,1,0:T(8,128)(2,1)S(1)}, bf16[16,32,128]{2,1,0:T(8,128)(2,1)S(1)}, u32[]{:S(2)}, u32[]{:S(2)}) collective-permute-start(bf16[16,32,128]{2,1,0:T(8,128)(2,1)S(1)} %copy.56), channel_id=1, source_target_pairs={{0,508},{4,0},{8,4},{12,8},{16,12},{20,16},{24,20},{28,24},{32,28}... | collective-permute-start | bytes 393224 | tf_op jit(solution)/shard_map/while/body/eval_jaxpr/ppermute | solution.py:13
  183.7 2.7 copy-start.7
  187.0 16.0 %collective-permute-start = (bf16[16,32,128]{2,1,0:T(8,128)(2,1)S(1)}, bf16[16,32,128]{2,1,0:T(8,128)(2,1)S(1)}, u32[]{:S(2)}, u32[]{:S(2)}) collective-permute-start(bf16[16,32,128]{2,1,0:T(8,128)(2,1)S(1)} %copy.56), channel_id=1, source_target_pairs={{0,508},{4,0},{8,4},{12,8},{16,12},{20,16},{24,20},{28,24},{32,28}... | collective-permute-start | bytes 393224 | tf_op jit(solution)/shard_map/while/body/eval_jaxpr/ppermute | solution.py:13
  200.3 2.7 copy-start.7
  203.7 1.2 copy-start.1
  206.2 0.8 copy-start.6
  208.2 1.9 copy-start.2
  211.7 3.3 %copy-start.9 = (f32[16]{0:T(128)S(1)}, f32[16]{0:T(128)}, u32[]{:S(2)}) copy-start(f32[16]{0:T(128)} %get-tuple-element.160) | copy-start | bytes 196
  (8 other events, 4.8 us)
Sparse Core Ops, SparseCore 0:
  213.0 57.2 reduce-scatter.1
where the time goes:
time: 280 us; the launch traced here: 279 us
  starting transfers between devices  86.1 us (31%)
  blocking collectives  50 us (18%)
  matrix products  40.1 us (14%)
  local copies, waits for them, and re-layouts  37.3 us (13%)
  waiting for transfers between devices  37.1 us (13%)
  between operations  15 us (5%)
  other arithmetic  11.9 us (4%)
    ppermute x9, starting transfers between devices, shifted(): lax.ppermute(array, axis, [(i, (i + by) % count) for i in range(count)])  86.1 us
    reduce_scatter x1, waiting for transfers between devices, body(): lax.psum_scatter(filtered, 'off', scatter_dimension=0, tiled=True)  33.3 us
    all_gather x1, blocking collectives, body(): own_block = lax.all_gather(coefficients, 'off', axis=1, tiled=True)  28.6 us
    unnamed x1, blocking collectives  21.4 us
    dot_general x8, matrix products, tile_terms(): jnp.einsum('ijc,jrc->irc', weight_imag, swapped, preferred_element_type=j...  19.2 us
    dot_general x8, matrix products, tile_terms(): jnp.dot(weights.reshape(row_count * row_count, -1), backward, precision=h...  7.98 us
    while x42, local copies, waits for them, and re-layouts  7.01 us
    unnamed x21, local copies, waits for them, and re-layouts  6.46 us
  transfers between devices with their start and end apart: 10, of which 3 were waited for; matrix products, arithmetic and copies ran while one was open for 22% of the time, Pallas kernels for 0%

commit v1 on v0

--- a/solution.py
+++ b/solution.py
@@ -71,7 +71,9 @@
 
 
 def body(coefficients):
-    own_block = lax.all_gather(coefficients, "off", axis=1, tiled=True)
+    own_block = jnp.concatenate(
+        lax.all_to_all(jnp.stack([coefficients] * lax.axis_size("off")), "off", 0, 0), axis=1
+    )
     own_inverse = inverse_norms(own_block)
     row_count, radial, angular = own_block.shape
     forward, backward = angle_tables(angular)

time: 280 us -> 257 us (0.918)
  blocking collectives: 50 us -> 24.3 us
  starting transfers between devices: 86.1 us -> 96.4 us
  matrix products: 40.1 us -> 31.9 us
  waiting for transfers between devices: 37.1 us -> 44.4 us
  local copies, waits for them, and re-layouts: 37.3 us -> 34.2 us
    all_gather x1 -> x0, blocking collectives: 28.6 us -> none  [body(): own_block = lax.all_gather(coefficients, 'off', axis=1, tiled=True)]
    all_to_all x0 -> x1, starting transfers between devices: none -> 16.6 us  [body(): lax.all_to_all(jnp.stack([coefficients] * lax.axis_size('off')), 'off', 0...]
    all_to_all x0 -> x1, waiting for transfers between devices: none -> 11.6 us  [body(): lax.all_to_all(jnp.stack([coefficients] * lax.axis_size('off')), 'off', 0...]
    ppermute x9, starting transfers between devices: 86.1 us -> 79.9 us  [shifted(): lax.ppermute(array, axis, [(i, (i + by) % count) for i in range(count)])]
    dot_general x8, matrix products: 7.98 us -> 2.1 us  [tile_terms(): jnp.dot(weights.reshape(row_count * row_count, -1), backward, precision=h...]
    reduce_scatter x1, waiting for transfers between devices: 33.3 us -> 29.3 us  [body(): lax.psum_scatter(filtered, 'off', scatter_dimension=0, tiled=True)]
    ppermute x2 -> x0, local copies, waits for them, and re-layouts: 3.87 us -> none  [shifted(): lax.ppermute(array, axis, [(i, (i + by) % count) for i in range(count)])]
    while x42 -> x70, local copies, waits for them, and re-layouts: 7.01 us -> 10.8 us
  transfers between devices with their start and end apart: 10 -> 11, of which waited for: 3 -> 4; matrix products, arithmetic and copies ran while one was open for 22% -> 22% of each run, Pallas kernels for 0% -> 0%
where the time goes in v1:
time: 257 us; the launch traced here: 256 us
  starting transfers between devices  96.4 us (38%)
  waiting for transfers between devices  44.4 us (17%)
  local copies, waits for them, and re-layouts  34.2 us (13%)
  matrix products  31.9 us (12%)
  blocking collectives  24.3 us (9%)
  between operations  15 us (6%)
  other arithmetic  9.26 us (4%)
    ppermute x9, starting transfers between devices, shifted(): lax.ppermute(array, axis, [(i, (i + by) % count) for i in range(count)])  79.9 us
    reduce_scatter x1, waiting for transfers between devices, body(): lax.psum_scatter(filtered, 'off', scatter_dimension=0, tiled=True)  29.3 us
    unnamed x1, blocking collectives  24.3 us
    dot_general x8, matrix products, tile_terms(): jnp.einsum('ijc,jrc->irc', weight_imag, swapped, preferred_element_type=j...  17.8 us
    all_to_all x1, starting transfers between devices, body(): lax.all_to_all(jnp.stack([coefficients] * lax.axis_size('off')), 'off', 0...  16.6 us
    all_to_all x1, waiting for transfers between devices, body(): lax.all_to_all(jnp.stack([coefficients] * lax.axis_size('off')), 'off', 0...  11.6 us
    while x70, local copies, waits for them, and re-layouts  10.8 us
  transfers between devices with their start and end apart: 11, of which 4 were waited for; matrix products, arithmetic and copies ran while one was open for 22% of the time, Pallas kernels for 0%

profile of v1, /device:TPU:1, one launch (start us, length us, event | category | flops | bytes accessed | tf_op | source)
XLA Modules:
  0.0 256.5 jit_solution(16513825102253351620)
XLA Ops:
  7.2 1.4 stack.2
  8.6 16.6 %all-to-all-start = ((bf16[4,16,8,128]{3,2,1,0:T(8,128)(2,1)}), bf16[4,16,8,128]{3,2,1,0:T(8,128)(2,1)S(1)}, u32[]{:S(2)}, u32[]{:S(2)}) async-start(bf16[4,16,8,128]{3,2,1,0:T(8,128)(2,1)} %stack.2), calls=%async_computation | async-start | bytes 262144 | tf_op jit(solution)/shard_map/all_to_all | solution.py:75
  25.9 11.6 %all-to-all-done = bf16[4,16,8,128]{3,2,1,0:T(8,128)(2,1)S(1)} async-done(((bf16[4,16,8,128]{3,2,1,0:T(8,128)(2,1)}), bf16[4,16,8,128]{3,2,1,0:T(8,128)(2,1)S(1)}, u32[]{:S(2)}, u32[]{:S(2)}) %all-to-all-start) | async-done | bytes 131104 | tf_op jit(solution)/shard_map/all_to_all | solution.py:75
  37.6 8.2 %collective-permute-start.1 = (bf16[16,32,128]{2,1,0:T(8,128)(2,1)S(1)}, bf16[16,32,128]{2,1,0:T(8,128)(2,1)S(1)}, u32[]{:S(2)}, u32[]{:S(2)}) collective-permute-start(bf16[16,32,128]{2,1,0:T(8,128)(2,1)S(1)} %bitcast.92), channel_id=1, source_target_pairs={{0,480},{4,484},{8,488},{12,492},{16,496},{20,500},{24,504},{28,50... | collective-permute-start | bytes 393224 | tf_op jit(solution)/shard_map/ppermute | solution.py:13
  47.8 3.7 %collective-permute-start.2 = (bf16[16,32,128]{2,1,0:T(8,128)(2,1)S(1)}, bf16[16,32,128]{2,1,0:T(8,128)(2,1)S(1)}, u32[]{:S(2)}, u32[]{:S(2)}) collective-permute-start(bf16[16,32,128]{2,1,0:T(8,128)(2,1)S(1)} %broadcast_select_fusion.1), channel_id=1, source_target_pairs={{0,448},{4,452},{8,456},{12,460},{16,464},{20,468},{24,472},{28,47... | collective-permute-start | bytes 393224 | tf_op jit(solution)/shard_map/ppermute | solution.py:13
  51.5 2.4 collective-permute-done.2
  53.9 129.3 %while.18 = (s32[]{:T(128)}, f32[16,32,128]{1,0,2:T(8,128)}, f32[16]{0:T(128)}, bf16[16,32,128]{2,1,0:T(8,128)(2,1)S(1)}, bf16[16,32,128]{1,0,2:T(8,128)(2,1)S(1...) while((s32[]{:T(128)}, f32[16,32,128]{1,0,2:T(8,128)}, ...), condition=%wide.region_4.5_spmd.clone, body=%wide.region_1.4_spmd.clone.sunk | while | flops 110216208 | bytes 6754670 | solution.py:99
  54.0 21.0 %collective-permute-start = (bf16[16,32,128]{2,1,0:T(8,128)(2,1)S(1)}, bf16[16,32,128]{2,1,0:T(8,128)(2,1)S(1)}, u32[]{:S(2)}, u32[]{:S(2)}) collective-permute-start(bf16[16,32,128]{2,1,0:T(8,128)(2,1)S(1)} %copy.66), channel_id=1, source_target_pairs={{0,508},{4,0},{8,4},{12,8},{16,12},{20,16},{24,20},{28,24},{32,28}... | collective-permute-start | bytes 393224 | tf_op jit(solution)/shard_map/while/body/eval_jaxpr/ppermute | solution.py:13
  80.1 1.4 fusion.94
  82.6 8.9 %collective-permute-start = (bf16[16,32,128]{2,1,0:T(8,128)(2,1)S(1)}, bf16[16,32,128]{2,1,0:T(8,128)(2,1)S(1)}, u32[]{:S(2)}, u32[]{:S(2)}) collective-permute-start(bf16[16,32,128]{2,1,0:T(8,128)(2,1)S(1)} %copy.66), channel_id=1, source_target_pairs={{0,508},{4,0},{8,4},{12,8},{16,12},{20,16},{24,20},{28,24},{32,28}... | collective-permute-start | bytes 393224 | tf_op jit(solution)/shard_map/while/body/eval_jaxpr/ppermute | solution.py:13
  96.7 2.7 %fusion.94 = f32[16,32,128]{1,0,2:T(8,128)} fusion(f32[16,32,128]{1,0,2:T(8,128)S(1)} %convolution_bitcast_fusion.11, bf16[16,16,128]{1,0,2:T(8,128)(2,1)S(1)} %copy.58, bf16[16,32,128]{1,0,2:T(8,128)(2,1)S(1)} %copy.53, f32[16,32,128]{1,0,2:T(8,128)} %get-tuple-element.347, pred[]{:T(512)S(6)} %compare.9), kind=kOutput, calls=%fused_computation.2.clone.1 | convolution fusion | flops 2293760 | bytes 983041 | tf_op jit(solution)/shard_map/while/body/eval_jaxpr/ijc,jrc->irc/dot_general | solution.py:67
  100.4 7.6 %collective-permute-start = (bf16[16,32,128]{2,1,0:T(8,128)(2,1)S(1)}, bf16[16,32,128]{2,1,0:T(8,128)(2,1)S(1)}, u32[]{:S(2)}, u32[]{:S(2)}) collective-permute-start(bf16[16,32,128]{2,1,0:T(8,128)(2,1)S(1)} %copy.66), channel_id=1, source_target_pairs={{0,508},{4,0},{8,4},{12,8},{16,12},{20,16},{24,20},{28,24},{32,28}... | collective-permute-start | bytes 393224 | tf_op jit(solution)/shard_map/while/body/eval_jaxpr/ppermute | solution.py:13
  113.2 2.7 %fusion.94 = f32[16,32,128]{1,0,2:T(8,128)} fusion(f32[16,32,128]{1,0,2:T(8,128)S(1)} %convolution_bitcast_fusion.11, bf16[16,16,128]{1,0,2:T(8,128)(2,1)S(1)} %copy.58, bf16[16,32,128]{1,0,2:T(8,128)(2,1)S(1)} %copy.53, f32[16,32,128]{1,0,2:T(8,128)} %get-tuple-element.347, pred[]{:T(512)S(6)} %compare.9), kind=kOutput, calls=%fused_computation.2.clone.1 | convolution fusion | flops 2293760 | bytes 983041 | tf_op jit(solution)/shard_map/while/body/eval_jaxpr/ijc,jrc->irc/dot_general | solution.py:67
  117.0 7.6 %collective-permute-start = (bf16[16,32,128]{2,1,0:T(8,128)(2,1)S(1)}, bf16[16,32,128]{2,1,0:T(8,128)(2,1)S(1)}, u32[]{:S(2)}, u32[]{:S(2)}) collective-permute-start(bf16[16,32,128]{2,1,0:T(8,128)(2,1)S(1)} %copy.66), channel_id=1, source_target_pairs={{0,508},{4,0},{8,4},{12,8},{16,12},{20,16},{24,20},{28,24},{32,28}... | collective-permute-start | bytes 393224 | tf_op jit(solution)/shard_map/while/body/eval_jaxpr/ppermute | solution.py:13
  129.8 2.7 %fusion.94 = f32[16,32,128]{1,0,2:T(8,128)} fusion(f32[16,32,128]{1,0,2:T(8,128)S(1)} %convolution_bitcast_fusion.11, bf16[16,16,128]{1,0,2:T(8,128)(2,1)S(1)} %copy.58, bf16[16,32,128]{1,0,2:T(8,128)(2,1)S(1)} %copy.53, f32[16,32,128]{1,0,2:T(8,128)} %get-tuple-element.347, pred[]{:T(512)S(6)} %compare.9), kind=kOutput, calls=%fused_computation.2.clone.1 | convolution fusion | flops 2293760 | bytes 983041 | tf_op jit(solution)/shard_map/while/body/eval_jaxpr/ijc,jrc->irc/dot_general | solution.py:67
  133.6 7.6 %collective-permute-start = (bf16[16,32,128]{2,1,0:T(8,128)(2,1)S(1)}, bf16[16,32,128]{2,1,0:T(8,128)(2,1)S(1)}, u32[]{:S(2)}, u32[]{:S(2)}) collective-permute-start(bf16[16,32,128]{2,1,0:T(8,128)(2,1)S(1)} %copy.66), channel_id=1, source_target_pairs={{0,508},{4,0},{8,4},{12,8},{16,12},{20,16},{24,20},{28,24},{32,28}... | collective-permute-start | bytes 393224 | tf_op jit(solution)/shard_map/while/body/eval_jaxpr/ppermute | solution.py:13
  146.3 2.7 %fusion.94 = f32[16,32,128]{1,0,2:T(8,128)} fusion(f32[16,32,128]{1,0,2:T(8,128)S(1)} %convolution_bitcast_fusion.11, bf16[16,16,128]{1,0,2:T(8,128)(2,1)S(1)} %copy.58, bf16[16,32,128]{1,0,2:T(8,128)(2,1)S(1)} %copy.53, f32[16,32,128]{1,0,2:T(8,128)} %get-tuple-element.347, pred[]{:T(512)S(6)} %compare.9), kind=kOutput, calls=%fused_computation.2.clone.1 | convolution fusion | flops 2293760 | bytes 983041 | tf_op jit(solution)/shard_map/while/body/eval_jaxpr/ijc,jrc->irc/dot_general | solution.py:67
  150.1 7.6 %collective-permute-start = (bf16[16,32,128]{2,1,0:T(8,128)(2,1)S(1)}, bf16[16,32,128]{2,1,0:T(8,128)(2,1)S(1)}, u32[]{:S(2)}, u32[]{:S(2)}) collective-permute-start(bf16[16,32,128]{2,1,0:T(8,128)(2,1)S(1)} %copy.66), channel_id=1, source_target_pairs={{0,508},{4,0},{8,4},{12,8},{16,12},{20,16},{24,20},{28,24},{32,28}... | collective-permute-start | bytes 393224 | tf_op jit(solution)/shard_map/while/body/eval_jaxpr/ppermute | solution.py:13
  162.9 2.7 %fusion.94 = f32[16,32,128]{1,0,2:T(8,128)} fusion(f32[16,32,128]{1,0,2:T(8,128)S(1)} %convolution_bitcast_fusion.11, bf16[16,16,128]{1,0,2:T(8,128)(2,1)S(1)} %copy.58, bf16[16,32,128]{1,0,2:T(8,128)(2,1)S(1)} %copy.53, f32[16,32,128]{1,0,2:T(8,128)} %get-tuple-element.347, pred[]{:T(512)S(6)} %compare.9), kind=kOutput, calls=%fused_computation.2.clone.1 | convolution fusion | flops 2293760 | bytes 983041 | tf_op jit(solution)/shard_map/while/body/eval_jaxpr/ijc,jrc->irc/dot_general | solution.py:67
  166.7 7.6 %collective-permute-start = (bf16[16,32,128]{2,1,0:T(8,128)(2,1)S(1)}, bf16[16,32,128]{2,1,0:T(8,128)(2,1)S(1)}, u32[]{:S(2)}, u32[]{:S(2)}) collective-permute-start(bf16[16,32,128]{2,1,0:T(8,128)(2,1)S(1)} %copy.66), channel_id=1, source_target_pairs={{0,508},{4,0},{8,4},{12,8},{16,12},{20,16},{24,20},{28,24},{32,28}... | collective-permute-start | bytes 393224 | tf_op jit(solution)/shard_map/while/body/eval_jaxpr/ppermute | solution.py:13
  179.4 2.7 %fusion.94 = f32[16,32,128]{1,0,2:T(8,128)} fusion(f32[16,32,128]{1,0,2:T(8,128)S(1)} %convolution_bitcast_fusion.11, bf16[16,16,128]{1,0,2:T(8,128)(2,1)S(1)} %copy.58, bf16[16,32,128]{1,0,2:T(8,128)(2,1)S(1)} %copy.53, f32[16,32,128]{1,0,2:T(8,128)} %get-tuple-element.347, pred[]{:T(512)S(6)} %compare.9), kind=kOutput, calls=%fused_computation.2.clone.1 | convolution fusion | flops 2293760 | bytes 983041 | tf_op jit(solution)/shard_map/while/body/eval_jaxpr/ijc,jrc->irc/dot_general | solution.py:67
  194.0 24.3 %all-reduce = f32[16]{0:T(128)S(1)} all-reduce(f32[16]{0:T(128)S(1)} %add.125), channel_id=3, replica_groups=mesh['blk'=128,'off'=4] {'off'}, use_global_device_ids=true, to_apply=%region_8.9.clone | all-reduce | flops 16 | bytes 128
  218.8 29.3 %reduce-scatter.2.cloned.1.call-done = f32[4,32,128]{2,1,0:T(8,128)} async-done(((f32[16,32,128]{2,1,0:T(8,128)}), f32[4,32,128]{2,1,0:T(8,128)}) %reduce-scatter.2.cloned.1.call-update) | async-done | bytes 65552 | tf_op jit(solution)/shard_map/reduce_scatter | solution.py:106
  248.1 1.5 broadcast_divide_fusion
  (278 shorter events, 56.1 us)
Async XLA Ops:
  8.6 28.9 %all-to-all-start = ((bf16[4,16,8,128]{3,2,1,0:T(8,128)(2,1)}), bf16[4,16,8,128]{3,2,1,0:T(8,128)(2,1)S(1)}, u32[]{:S(2)}, u32[]{:S(2)}) async-start(bf16[4,16,8,128]{3,2,1,0:T(8,128)(2,1)} %stack.2), calls=%async_computation | async-start | bytes 262144 | tf_op jit(solution)/shard_map/all_to_all | solution.py:75
  25.2 222.9 %reduce-scatter.2.cloned.1.call-start = ((), (), s32[]{:S(2)}) async-start(), calls=%async_computation.2 | async-start | bytes 327680 | tf_op jit(solution)/shard_map/reduce_scatter | solution.py:106
  37.6 10.2 %collective-permute-start.1 = (bf16[16,32,128]{2,1,0:T(8,128)(2,1)S(1)}, bf16[16,32,128]{2,1,0:T(8,128)(2,1)S(1)}, u32[]{:S(2)}, u32[]{:S(2)}) collective-permute-start(bf16[16,32,128]{2,1,0:T(8,128)(2,1)S(1)} %bitcast.92), channel_id=1, source_target_pairs={{0,480},{4,484},{8,488},{12,492},{16,496},{20,500},{24,504},{28,50... | collective-permute-start | bytes 393224 | tf_op jit(solution)/shard_map/ppermute | solution.py:13
  47.8 6.1 %collective-permute-start.2 = (bf16[16,32,128]{2,1,0:T(8,128)(2,1)S(1)}, bf16[16,32,128]{2,1,0:T(8,128)(2,1)S(1)}, u32[]{:S(2)}, u32[]{:S(2)}) collective-permute-start(bf16[16,32,128]{2,1,0:T(8,128)(2,1)S(1)} %broadcast_select_fusion.1), channel_id=1, source_target_pairs={{0,448},{4,452},{8,456},{12,460},{16,464},{20,468},{24,472},{28,47... | collective-permute-start | bytes 393224 | tf_op jit(solution)/shard_map/ppermute | solution.py:13
  53.9 24.2 %copy-start.1 = (f32[128,128]{1,0:T(8,128)}, f32[128,128]{1,0:T(8,128)S(1)}, u32[]{:S(2)}) copy-start(f32[128,128]{1,0:T(8,128)S(1)} %get-tuple-element.365) | copy-start | bytes 196612 | tf_op jit(solution)/shard_map/while
  54.0 28.2 %collective-permute-start = (bf16[16,32,128]{2,1,0:T(8,128)(2,1)S(1)}, bf16[16,32,128]{2,1,0:T(8,128)(2,1)S(1)}, u32[]{:S(2)}, u32[]{:S(2)}) collective-permute-start(bf16[16,32,128]{2,1,0:T(8,128)(2,1)S(1)} %copy.66), channel_id=1, source_target_pairs={{0,508},{4,0},{8,4},{12,8},{16,12},{20,16},{24,20},{28,24},{32,28}... | collective-permute-start | bytes 393224 | tf_op jit(solution)/shard_map/while/body/eval_jaxpr/ppermute | solution.py:13
  82.6 12.1 %copy-start.1 = (f32[128,128]{1,0:T(8,128)}, f32[128,128]{1,0:T(8,128)S(1)}, u32[]{:S(2)}) copy-start(f32[128,128]{1,0:T(8,128)S(1)} %get-tuple-element.365) | copy-start | bytes 196612 | tf_op jit(solution)/shard_map/while
  82.6 17.3 %collective-permute-start = (bf16[16,32,128]{2,1,0:T(8,128)(2,1)S(1)}, bf16[16,32,128]{2,1,0:T(8,128)(2,1)S(1)}, u32[]{:S(2)}, u32[]{:S(2)}) collective-permute-start(bf16[16,32,128]{2,1,0:T(8,128)(2,1)S(1)} %copy.66), channel_id=1, source_target_pairs={{0,508},{4,0},{8,4},{12,8},{16,12},{20,16},{24,20},{28,24},{32,28}... | collective-permute-start | bytes 393224 | tf_op jit(solution)/shard_map/while/body/eval_jaxpr/ppermute | solution.py:13
  96.6 3.8 %copy-start.2 = (f32[128,128]{1,0:T(8,128)S(1)}, f32[128,128]{1,0:T(8,128)}, u32[]{:S(2)}) copy-start(f32[128,128]{1,0:T(8,128)} %copy-done.1) | copy-start | bytes 196612 | tf_op jit(solution)/shard_map/while
  100.4 10.8 %copy-start.1 = (f32[128,128]{1,0:T(8,128)}, f32[128,128]{1,0:T(8,128)S(1)}, u32[]{:S(2)}) copy-start(f32[128,128]{1,0:T(8,128)S(1)} %get-tuple-element.365) | copy-start | bytes 196612 | tf_op jit(solution)/shard_map/while
  100.4 16.0 %collective-permute-start = (bf16[16,32,128]{2,1,0:T(8,128)(2,1)S(1)}, bf16[16,32,128]{2,1,0:T(8,128)(2,1)S(1)}, u32[]{:S(2)}, u32[]{:S(2)}) collective-permute-start(bf16[16,32,128]{2,1,0:T(8,128)(2,1)S(1)} %copy.66), channel_id=1, source_target_pairs={{0,508},{4,0},{8,4},{12,8},{16,12},{20,16},{24,20},{28,24},{32,28}... | collective-permute-start | bytes 393224 | tf_op jit(solution)/shard_map/while/body/eval_jaxpr/ppermute | solution.py:13
  113.2 3.8 %copy-start.2 = (f32[128,128]{1,0:T(8,128)S(1)}, f32[128,128]{1,0:T(8,128)}, u32[]{:S(2)}) copy-start(f32[128,128]{1,0:T(8,128)} %copy-done.1) | copy-start | bytes 196612 | tf_op jit(solution)/shard_map/while
  117.0 10.8 %copy-start.1 = (f32[128,128]{1,0:T(8,128)}, f32[128,128]{1,0:T(8,128)S(1)}, u32[]{:S(2)}) copy-start(f32[128,128]{1,0:T(8,128)S(1)} %get-tuple-element.365) | copy-start | bytes 196612 | tf_op jit(solution)/shard_map/while
  117.0 16.0 %collective-permute-start = (bf16[16,32,128]{2,1,0:T(8,128)(2,1)S(1)}, bf16[16,32,128]{2,1,0:T(8,128)(2,1)S(1)}, u32[]{:S(2)}, u32[]{:S(2)}) collective-permute-start(bf16[16,32,128]{2,1,0:T(8,128)(2,1)S(1)} %copy.66), channel_id=1, source_target_pairs={{0,508},{4,0},{8,4},{12,8},{16,12},{20,16},{24,20},{28,24},{32,28}... | collective-permute-start | bytes 393224 | tf_op jit(solution)/shard_map/while/body/eval_jaxpr/ppermute | solution.py:13
  129.8 3.8 %copy-start.2 = (f32[128,128]{1,0:T(8,128)S(1)}, f32[128,128]{1,0:T(8,128)}, u32[]{:S(2)}) copy-start(f32[128,128]{1,0:T(8,128)} %copy-done.1) | copy-start | bytes 196612 | tf_op jit(solution)/shard_map/while
  133.5 10.8 %copy-start.1 = (f32[128,128]{1,0:T(8,128)}, f32[128,128]{1,0:T(8,128)S(1)}, u32[]{:S(2)}) copy-start(f32[128,128]{1,0:T(8,128)S(1)} %get-tuple-element.365) | copy-start | bytes 196612 | tf_op jit(solution)/shard_map/while
  133.6 16.0 %collective-permute-start = (bf16[16,32,128]{2,1,0:T(8,128)(2,1)S(1)}, bf16[16,32,128]{2,1,0:T(8,128)(2,1)S(1)}, u32[]{:S(2)}, u32[]{:S(2)}) collective-permute-start(bf16[16,32,128]{2,1,0:T(8,128)(2,1)S(1)} %copy.66), channel_id=1, source_target_pairs={{0,508},{4,0},{8,4},{12,8},{16,12},{20,16},{24,20},{28,24},{32,28}... | collective-permute-start | bytes 393224 | tf_op jit(solution)/shard_map/while/body/eval_jaxpr/ppermute | solution.py:13
  146.3 3.8 %copy-start.2 = (f32[128,128]{1,0:T(8,128)S(1)}, f32[128,128]{1,0:T(8,128)}, u32[]{:S(2)}) copy-start(f32[128,128]{1,0:T(8,128)} %copy-done.1) | copy-start | bytes 196612 | tf_op jit(solution)/shard_map/while
  150.1 10.8 %copy-start.1 = (f32[128,128]{1,0:T(8,128)}, f32[128,128]{1,0:T(8,128)S(1)}, u32[]{:S(2)}) copy-start(f32[128,128]{1,0:T(8,128)S(1)} %get-tuple-element.365) | copy-start | bytes 196612 | tf_op jit(solution)/shard_map/while
  150.1 16.0 %collective-permute-start = (bf16[16,32,128]{2,1,0:T(8,128)(2,1)S(1)}, bf16[16,32,128]{2,1,0:T(8,128)(2,1)S(1)}, u32[]{:S(2)}, u32[]{:S(2)}) collective-permute-start(bf16[16,32,128]{2,1,0:T(8,128)(2,1)S(1)} %copy.66), channel_id=1, source_target_pairs={{0,508},{4,0},{8,4},{12,8},{16,12},{20,16},{24,20},{28,24},{32,28}... | collective-permute-start | bytes 393224 | tf_op jit(solution)/shard_map/while/body/eval_jaxpr/ppermute | solution.py:13
  162.9 3.8 %copy-start.2 = (f32[128,128]{1,0:T(8,128)S(1)}, f32[128,128]{1,0:T(8,128)}, u32[]{:S(2)}) copy-start(f32[128,128]{1,0:T(8,128)} %copy-done.1) | copy-start | bytes 196612 | tf_op jit(solution)/shard_map/while
  166.7 10.8 %copy-start.1 = (f32[128,128]{1,0:T(8,128)}, f32[128,128]{1,0:T(8,128)S(1)}, u32[]{:S(2)}) copy-start(f32[128,128]{1,0:T(8,128)S(1)} %get-tuple-element.365) | copy-start | bytes 196612 | tf_op jit(solution)/shard_map/while
  166.7 16.0 %collective-permute-start = (bf16[16,32,128]{2,1,0:T(8,128)(2,1)S(1)}, bf16[16,32,128]{2,1,0:T(8,128)(2,1)S(1)}, u32[]{:S(2)}, u32[]{:S(2)}) collective-permute-start(bf16[16,32,128]{2,1,0:T(8,128)(2,1)S(1)} %copy.66), channel_id=1, source_target_pairs={{0,508},{4,0},{8,4},{12,8},{16,12},{20,16},{24,20},{28,24},{32,28}... | collective-permute-start | bytes 393224 | tf_op jit(solution)/shard_map/while/body/eval_jaxpr/ppermute | solution.py:13
  179.4 3.8 %copy-start.2 = (f32[128,128]{1,0:T(8,128)S(1)}, f32[128,128]{1,0:T(8,128)}, u32[]{:S(2)}) copy-start(f32[128,128]{1,0:T(8,128)} %copy-done.1) | copy-start | bytes 196612 | tf_op jit(solution)/shard_map/while
  (21 other events, 14.8 us)
Sparse Core Ops, SparseCore 0:
  191.4 56.7 reduce-scatter.1
